TPU v7x, 32 devices: a whole 2x2x4 slice. The times are simulated.
32 devices in a mesh: team: 2 (over core), obs: 4 (over z), grid: 4 (over y, x).
Axes of the slice: x: 2, y: 2, z: 4, core: 2. Of those that a mesh axis runs over, the one named last changes fastest.
Arguments:
- design_panel: bfloat16 [8192, 1024], P('obs', ('team', 'grid')), may hold values from -6 to 6
- design_front: bfloat16 [8192, 6144], P('obs', 'grid'), may hold values from -6 to 6
- arc_ids: int32 [8192], P('obs'), may hold values from 0 to 127
- arc_weight: float32 [128], replicated, may hold values from 0.5 to 2
- row_counts: int32 [4], P('obs'), may hold values from 128 to 2048, as said below
- panel_inverse: float32 [1024, 1024], P(('team', 'obs')), may hold values from -6.525546e-05 to 0.0020539933
- front: float32 [6144, 6144], P(('team', 'obs'), 'grid'), may hold values from -1.2 to 21.2
Outputs:
- factor_row: float32 [1024, 6144], P(('team', 'obs'), 'grid')
- front_next: float32 [6144, 6144], P(('team', 'obs'), 'grid')
Inputs may be any that keep to these rules, and one draw needn't show every extreme that they name: `row_counts`: every count is a multiple of 128, and in every draw some shard's count equals 2048.
All inputs are finite; a program needn't handle non-finite values.
Results may differ from a plain program's by a relative error of at most 0.0035.
Values may be sent and summed in bfloat16 or wider, within the bound.
A program may use at most 64 MiB of HBM per device.

v0:
```python
import jax
import jax.numpy as jnp
from jax import lax
from jax.sharding import PartitionSpec as P


def live_weights(arc_ids, arc_weight, row_counts):
    row_total = arc_ids.shape[0]
    arc_total = arc_weight.shape[0]
    hit = arc_ids[:, None] == lax.broadcasted_iota(jnp.int32, (row_total, arc_total), 1)
    looked = jnp.sum(jnp.where(hit, arc_weight[None, :], 0.0), axis=1)
    is_live = lax.broadcasted_iota(jnp.int32, (row_total,), 0) < row_counts[0]
    return looked * is_live.astype(jnp.float32)


def contract_rows(left, right):
    return lax.dot_general(
        left, right, (((0,), (0,)), ((), ())), preferred_element_type=jnp.float32
    )


def local(design_panel, design_front, arc_ids, arc_weight, row_counts, panel_inverse, front):
    high = lax.reduce_precision(panel_inverse, 8, 7)
    split = jnp.concatenate([high, panel_inverse - high], axis=1).astype(jnp.bfloat16)
    inverse_whole = lax.all_gather(split, ("team", "obs"), axis=0, tiled=True)
    weights = live_weights(arc_ids, arc_weight, row_counts)
    scaled_front = (design_front.astype(jnp.float32) * weights[:, None]).astype(jnp.bfloat16)
    panel_piece = lax.all_gather(design_panel, "grid", axis=1, tiled=True)
    partial_value = contract_rows(panel_piece, scaled_front)
    slab_rows = panel_inverse.shape[0]
    place_index = lax.axis_index(("team", "obs"))
    block_part = lax.psum_scatter(partial_value, "obs", scatter_dimension=0, tiled=True)
    block_part = block_part.astype(jnp.bfloat16)
    block_whole = lax.all_gather(block_part, ("team", "obs"), axis=0, tiled=True)
    factor_cols = jnp.dot(
        inverse_whole,
        jnp.concatenate([block_whole, block_whole], axis=0),
        preferred_element_type=jnp.float32,
    )
    factor_part = lax.dynamic_slice_in_dim(factor_cols, place_index * slab_rows, slab_rows, 0)
    factor_cols = factor_cols.astype(jnp.bfloat16)
    tile_rows = front.shape[0]
    tile_ratio = factor_cols.shape[1] // tile_rows
    offset = place_index % tile_ratio * tile_rows
    own_slice = lax.dynamic_slice_in_dim(factor_cols, offset, tile_rows, 1)
    kept = jnp.where(lax.axis_index("grid") == place_index // tile_ratio, own_slice, 0)
    factor_rows = lax.psum(kept.astype(jnp.bfloat16), "grid")
    return (factor_part, front - contract_rows(factor_rows, factor_cols))


def solution(mesh):
    placed = (
        P("obs", ("team", "grid")),
        P("obs", "grid"),
        P("obs"),
        P(),
        P("obs"),
        P(("team", "obs"), None),
        P(("team", "obs"), "grid"),
    )
    return jax.shard_map(
        local,
        mesh=mesh,
        in_specs=placed,
        out_specs=(P(("team", "obs"), "grid"), P(("team", "obs"), "grid")),
        check_vma=False,
    )
```

profile of v0, /device:TPU:0, one launch (start us, length us, event | category | flops | bytes accessed | tf_op | source)
XLA Modules:
  0.0 278.6 jit_solution(38822958594479527)
XLA Ops:
  8.0 0.0 all-gather.6.cloned.1.call-start
  8.0 0.7 all-gather.6.cloned.1.call-update
  8.7 0.0 reduce-scatter.2.cloned.1.call-start
  9.4 1.3 select_reduce_fusion
  10.8 0.0 copy-start
  10.8 37.6 %all-gather.6.cloned.1.call-done = bf16[2048,512]{1,0:T(8,128)(2,1)} async-done(((bf16[2048,128]{1,0:T(8,128)(2,1)}), bf16[2048,512]{1,0:T(8,128)(2,1)}) %all-gather.6.cloned.1.call-update) | async-done | bytes 2097168 | tf_op jit(solution)/shard_map/all_gather | solution.py:28
  48.4 8.6 %fusion.6 = f32[512,1536]{0,1:T(8,128)} fusion(bf16[2048,512]{1,0:T(8,128)(2,1)} %all-gather.6.cloned.1.call-done, bf16[2048,1536]{1,0:T(8,128)(2,1)} %param.8, f32[2048]{0:T(1024)S(1)} %fusion.8), kind=kOutput, calls=%fused_computation.8 | convolution fusion | flops 3230662656 | bytes 11542528 | tf_op jit(solution)/shard_map/dot_general | solution.py:17
  57.1 0.0 reduce-scatter.2.cloned.1.call-update
  57.1 0.0 all-gather.4.cloned.1.call-start
  57.2 0.0 copy-done
  57.2 0.1 reduce-precision_convert_fusion
  57.3 0.8 pad_maximum_fusion
  58.1 0.0 all-gather.4.cloned.1.call-update
  58.1 0.0 all-gather.8.cloned.1.call-start
  58.2 83.4 %reduce-scatter.2.cloned.1.call-done = f32[128,1536]{0,1:T(8,128)} async-done(((f32[512,1536]{0,1:T(8,128)}), f32[128,1536]{0,1:T(8,128)}) %reduce-scatter.2.cloned.1.call-update) | async-done | bytes 786448 | tf_op jit(solution)/shard_map/reduce_scatter | solution.py:32
  141.5 1.9 convert_element_type.18
  143.5 0.0 all-gather.8.cloned.1.call-update
  143.5 0.0 all-reduce.2.cloned.1.call-start
  143.6 7.5 %all-gather.4.cloned.1.call-done = bf16[1024,2048]{1,0:T(8,128)(2,1)} async-done(((bf16[128,2048]{1,0:T(8,128)(2,1)}), bf16[1024,2048]{1,0:T(8,128)(2,1)}) %all-gather.4.cloned.1.call-update) | async-done | bytes 4194320 | tf_op jit(solution)/shard_map/all_gather | solution.py:25
  151.1 41.5 %all-gather.8.cloned.1.call-done = bf16[1024,1536]{0,1:T(8,128)(2,1)} async-done(((bf16[128,1536]{0,1:T(8,128)(2,1)}), bf16[1024,1536]{0,1:T(8,128)(2,1)}) %all-gather.8.cloned.1.call-update) | async-done | bytes 3145744 | tf_op jit(solution)/shard_map/all_gather | solution.py:34
  192.6 11.9 %fusion.10 = (bf16[1024,1536]{1,0:T(8,128)(2,1)S(1)}, f32[1024,1536]{1,0:T(8,128)}) fusion(bf16[1024,2048]{1,0:T(8,128)(2,1)} %all-gather.4.cloned.1.call-done, bf16[1024,1536]{0,1:T(8,128)(2,1)} %all-gather.8.cloned.1.call-done), kind=kOutput, calls=%fused_computation.20 | convolution fusion | flops 6456606720 | bytes 16777216 | tf_op jit(solution)/shard_map/dot_general | solution.py:35
  204.5 1.4 dynamic-slice_select_fusion
  205.9 0.0 all-reduce.2.cloned.1.call-update
  206.0 2.1 constant_dynamic-slice_fusion
  208.0 57.0 %all-reduce.2.cloned.1.call-done = bf16[1024,768]{1,0:T(8,128)(2,1)} async-done(((bf16[1024,768]{1,0:T(8,128)(2,1)}), bf16[1024,768]{1,0:T(8,128)(2,1)}) %all-reduce.2.cloned.1.call-update) | async-done | bytes 1572880 | tf_op jit(solution)/shard_map/psum | solution.py:47
  265.1 6.4 %convolution_subtract_fusion = f32[768,1536]{1,0:T(8,128)} fusion(f32[768,1536]{1,0:T(8,128)} %param.13, bf16[1024,768]{1,0:T(8,128)(2,1)} %all-reduce.2.cloned.1.call-done, bf16[1024,1536]{1,0:T(8,128)(2,1)S(1)} %get-tuple-element.4), kind=kOutput, calls=%fused_computation.7 | convolution fusion | flops 2417098752 | bytes 14155776 | tf_op jit(solution)/shard_map/dot_general | solution.py:17
  (1 shorter events, 0.0 us)
Async XLA Ops:
  8.0 40.4 %all-gather.6.cloned.1.call-start = ((), (), s32[]{:S(2)}) async-start(), calls=%async_computation.2 | async-start | bytes 2621440 | tf_op jit(solution)/shard_map/all_gather | solution.py:28
  8.7 132.8 %reduce-scatter.2.cloned.1.call-start = ((), (), s32[]{:S(2)}) async-start(), calls=%async_computation.3 | async-start | bytes 3932160 | tf_op jit(solution)/shard_map/reduce_scatter | solution.py:32
  10.8 46.4 %copy-start = (f32[128,1024]{1,0:T(8,128)S(1)}, f32[128,1024]{1,0:T(8,128)}, u32[]{:S(2)}) copy-start(f32[128,1024]{1,0:T(8,128)} %param.12) | copy-start | bytes 1572868
  57.1 94.0 %all-gather.4.cloned.1.call-start = ((), (), s32[]{:S(2)}) async-start(), calls=%async_computation.1 | async-start | bytes 4718592 | tf_op jit(solution)/shard_map/all_gather | solution.py:25
  58.1 134.5 %all-gather.8.cloned.1.call-start = ((), (), s32[]{:S(2)}) async-start(), calls=%async_computation.4 | async-start | bytes 3538944 | tf_op jit(solution)/shard_map/all_gather | solution.py:34
  143.5 121.6 %all-reduce.2.cloned.1.call-start = ((), (), s32[]{:S(2)}) async-start(), calls=%async_computation.5 | async-start | bytes 3145728 | tf_op jit(solution)/shard_map/psum | solution.py:47
Sparse Core Ops, SparseCore 0:
  10.6 37.7 all-gather.5
  57.2 84.2 reduce-scatter.1
  206.1 58.9 all-reduce.1
Sparse Core Ops, SparseCore 1:
  59.8 91.3 all-gather.3
  153.1 39.4 all-gather.7
where the time goes:
time: 279 us
  waiting for transfers between devices  228 us (82%)
  matrix products  27 us (10%)
  between operations  15.9 us (6%)
  other arithmetic  5.59 us (2%)
    reduce_scatter x1, waiting for transfers between devices, local(): lax.psum_scatter(partial_value, 'obs', scatter_dimension=0, tiled=True)  83.4 us
    psum x1, waiting for transfers between devices, local(): factor_rows = lax.psum(kept.astype(jnp.bfloat16), 'grid')  57 us
    all_gather x1, waiting for transfers between devices, local(): lax.all_gather(block_part, ('team', 'obs'), axis=0, tiled=True)  41.5 us
    all_gather x1, waiting for transfers between devices, local(): panel_piece = lax.all_gather(design_panel, 'grid', axis=1, tiled=True)  37.6 us
    dot_general x2, matrix products, contract_rows(): lax.dot_general(left, right, (((0,), (0,)), ((), ())), preferred_element_...  15.1 us
    dot_general x1, matrix products, local(): jnp.dot(inverse_whole, jnp.concatenate([block_whole, block_whole], axis=0...  11.9 us
    all_gather x1, waiting for transfers between devices, local(): inverse_whole = lax.all_gather(split, ('team', 'obs'), axis=0, tiled=True)  7.5 us
  transfers between devices with their start and end apart: 5, of which 5 were waited for; matrix products, arithmetic and copies ran while one was open for 2% of the time, Pallas kernels for 0%

commit v1 on v0

--- a/solution.py
+++ b/solution.py
@@ -25,7 +25,7 @@
     inverse_whole = lax.all_gather(split, ("team", "obs"), axis=0, tiled=True)
     weights = live_weights(arc_ids, arc_weight, row_counts)
     scaled_front = (design_front.astype(jnp.float32) * weights[:, None]).astype(jnp.bfloat16)
-    panel_piece = lax.all_gather(design_panel, "grid", axis=1, tiled=True)
+    panel_piece = jnp.concatenate(lax.all_gather(design_panel, "grid"), axis=1)
     partial_value = contract_rows(panel_piece, scaled_front)
     slab_rows = panel_inverse.shape[0]
     place_index = lax.axis_index(("team", "obs"))

time: 279 us -> 282 us (1.011)
  local copies, waits for them, and re-layouts: 2.08 us -> 5.01 us
    reshape x0 -> x1, local copies, waits for them, and re-layouts: none -> 2.93 us  [local(): panel_piece = jnp.concatenate(lax.all_gather(design_panel, 'grid'), axis=1)]
where the time goes in v1:
time: 282 us
  waiting for transfers between devices  228 us (81%)
  matrix products  26.8 us (10%)
  between operations  15.9 us (6%)
  other arithmetic  5.59 us (2%)
  local copies, waits for them, and re-layouts  5.01 us (2%)
    reduce_scatter x1, waiting for transfers between devices, local(): lax.psum_scatter(partial_value, 'obs', scatter_dimension=0, tiled=True)  83.4 us
    psum x1, waiting for transfers between devices, local(): factor_rows = lax.psum(kept.astype(jnp.bfloat16), 'grid')  57 us
    all_gather x1, waiting for transfers between devices, local(): lax.all_gather(block_part, ('team', 'obs'), axis=0, tiled=True)  41.5 us
    all_gather x1, waiting for transfers between devices, local(): panel_piece = jnp.concatenate(lax.all_gather(design_panel, 'grid'), axis=1)  37.8 us
    dot_general x2, matrix products, contract_rows(): lax.dot_general(left, right, (((0,), (0,)), ((), ())), preferred_element_...  14.9 us
    dot_general x1, matrix products, local(): jnp.dot(inverse_whole, jnp.concatenate([block_whole, block_whole], axis=0...  11.9 us
    all_gather x1, waiting for transfers between devices, local(): inverse_whole = lax.all_gather(split, ('team', 'obs'), axis=0, tiled=True)  7.5 us
  transfers between devices with their start and end apart: 5, of which 5 were waited for; matrix products, arithmetic and copies ran while one was open for 2% of the time, Pallas kernels for 0%

profile of v1, /device:TPU:0, one launch (start us, length us, event | category | flops | bytes accessed | tf_op | source)
XLA Modules:
  0.0 281.5 jit_solution(11901904967965013858)
XLA Ops:
  8.0 0.0 all-gather.9.cloned.1.call-start
  8.0 0.7 all-gather.9.cloned.1.call-update
  8.7 0.0 reduce-scatter.2.cloned.1.call-start
  9.4 1.3 select_reduce_fusion
  10.8 37.8 %all-gather.9.cloned.1.call-done = bf16[8192,128]{1,0:T(8,128)(2,1)} async-done(((bf16[2048,128]{1,0:T(8,128)(2,1)}), bf16[8192,128]{1,0:T(8,128)(2,1)}) %all-gather.9.cloned.1.call-update) | async-done | bytes 2097168 | tf_op jit(solution)/shard_map/all_gather | solution.py:28
  48.6 2.9 %copy.10 = bf16[2048,4,128]{0,2,1:T(8,128)(2,1)S(1)} copy(bf16[2048,4,128]{2,0,1:T(8,128)(2,1)} %bitcast.12) | data formatting | bytes 4194304 | tf_op jit(solution)/shard_map/reshape | solution.py:28
  51.5 0.0 copy-start
  51.5 8.4 %fusion.6 = f32[512,1536]{0,1:T(8,128)} fusion(bf16[2048,512]{0,1:T(8,128)(2,1)S(1)} %bitcast.13, bf16[2048,1536]{1,0:T(8,128)(2,1)} %param.8, f32[2048]{0:T(1024)S(1)} %fusion.8), kind=kOutput, calls=%fused_computation.8 | convolution fusion | flops 3230662656 | bytes 11542528 | tf_op jit(solution)/shard_map/dot_general | solution.py:17
  60.0 0.0 reduce-scatter.2.cloned.1.call-update
  60.0 0.0 all-gather.5.cloned.1.call-start
  60.0 0.0 copy-done
  60.1 0.1 reduce-precision_convert_fusion
  60.1 0.8 pad_maximum_fusion
  61.0 0.0 all-gather.5.cloned.1.call-update
  61.0 0.0 all-gather.7.cloned.1.call-start
  61.1 83.4 %reduce-scatter.2.cloned.1.call-done = f32[128,1536]{0,1:T(8,128)} async-done(((f32[512,1536]{0,1:T(8,128)}), f32[128,1536]{0,1:T(8,128)}) %reduce-scatter.2.cloned.1.call-update) | async-done | bytes 786448 | tf_op jit(solution)/shard_map/reduce_scatter | solution.py:32
  144.4 1.9 convert_element_type.18
  146.4 0.0 all-gather.7.cloned.1.call-update
  146.4 0.0 all-reduce.2.cloned.1.call-start
  146.5 7.5 %all-gather.5.cloned.1.call-done = bf16[1024,2048]{1,0:T(8,128)(2,1)} async-done(((bf16[128,2048]{1,0:T(8,128)(2,1)}), bf16[1024,2048]{1,0:T(8,128)(2,1)}) %all-gather.5.cloned.1.call-update) | async-done | bytes 4194320 | tf_op jit(solution)/shard_map/all_gather | solution.py:25
  154.0 41.5 %all-gather.7.cloned.1.call-done = bf16[1024,1536]{0,1:T(8,128)(2,1)} async-done(((bf16[128,1536]{0,1:T(8,128)(2,1)}), bf16[1024,1536]{0,1:T(8,128)(2,1)}) %all-gather.7.cloned.1.call-update) | async-done | bytes 3145744 | tf_op jit(solution)/shard_map/all_gather | solution.py:34
  195.5 11.9 %fusion.10 = (bf16[1024,1536]{1,0:T(8,128)(2,1)S(1)}, f32[1024,1536]{1,0:T(8,128)}) fusion(bf16[1024,2048]{1,0:T(8,128)(2,1)} %all-gather.5.cloned.1.call-done, bf16[1024,1536]{0,1:T(8,128)(2,1)} %all-gather.7.cloned.1.call-done), kind=kOutput, calls=%fused_computation.20 | convolution fusion | flops 6456606720 | bytes 16777216 | tf_op jit(solution)/shard_map/dot_general | solution.py:35
  207.4 1.4 dynamic-slice_select_fusion
  208.8 0.0 all-reduce.2.cloned.1.call-update
  208.9 2.1 constant_dynamic-slice_fusion
  210.9 57.0 %all-reduce.2.cloned.1.call-done = bf16[1024,768]{1,0:T(8,128)(2,1)} async-done(((bf16[1024,768]{1,0:T(8,128)(2,1)}), bf16[1024,768]{1,0:T(8,128)(2,1)}) %all-reduce.2.cloned.1.call-update) | async-done | bytes 1572880 | tf_op jit(solution)/shard_map/psum | solution.py:47
  267.9 6.4 %convolution_subtract_fusion = f32[768,1536]{1,0:T(8,128)} fusion(f32[768,1536]{1,0:T(8,128)} %param.13, bf16[1024,768]{1,0:T(8,128)(2,1)} %all-reduce.2.cloned.1.call-done, bf16[1024,1536]{1,0:T(8,128)(2,1)S(1)} %get-tuple-element.4), kind=kOutput, calls=%fused_computation.7 | convolution fusion | flops 2417098752 | bytes 14155776 | tf_op jit(solution)/shard_map/dot_general | solution.py:17
  (1 shorter events, 0.0 us)
Async XLA Ops:
  8.0 40.6 %all-gather.9.cloned.1.call-start = ((), (), s32[]{:S(2)}) async-start(), calls=%async_computation.5 | async-start | bytes 2621440 | tf_op jit(solution)/shard_map/all_gather | solution.py:28
  8.7 135.7 %reduce-scatter.2.cloned.1.call-start = ((), (), s32[]{:S(2)}) async-start(), calls=%async_computation.2 | async-start | bytes 3932160 | tf_op jit(solution)/shard_map/reduce_scatter | solution.py:32
  51.5 8.5 %copy-start = (f32[128,1024]{1,0:T(8,128)S(1)}, f32[128,1024]{1,0:T(8,128)}, u32[]{:S(2)}) copy-start(f32[128,1024]{1,0:T(8,128)} %param.12) | copy-start | bytes 1572868
  60.0 94.0 %all-gather.5.cloned.1.call-start = ((), (), s32[]{:S(2)}) async-start(), calls=%async_computation.1 | async-start | bytes 4718592 | tf_op jit(solution)/shard_map/all_gather | solution.py:25
  61.0 134.5 %all-gather.7.cloned.1.call-start = ((), (), s32[]{:S(2)}) async-start(), calls=%async_computation.3 | async-start | bytes 3538944 | tf_op jit(solution)/shard_map/all_gather | solution.py:34
  146.4 121.6 %all-reduce.2.cloned.1.call-start = ((), (), s32[]{:S(2)}) async-start(), calls=%async_computation.4 | async-start | bytes 3145728 | tf_op jit(solution)/shard_map/psum | solution.py:47
Sparse Core Ops, SparseCore 0:
  10.6 37.8 all-gather.8
  60.1 84.2 reduce-scatter.1
  209.0 58.9 all-reduce.1
Sparse Core Ops, SparseCore 1:
  62.7 91.3 all-gather.4
  156.0 39.4 all-gather.6

commit v2 on v0

--- a/solution.py
+++ b/solution.py
@@ -44,7 +44,7 @@
     offset = place_index % tile_ratio * tile_rows
     own_slice = lax.dynamic_slice_in_dim(factor_cols, offset, tile_rows, 1)
     kept = jnp.where(lax.axis_index("grid") == place_index // tile_ratio, own_slice, 0)
-    factor_rows = lax.psum(kept.astype(jnp.bfloat16), "grid")
+    factor_rows = jnp.sum(lax.all_gather(kept.astype(jnp.bfloat16), "grid"), axis=0)
     return (factor_part, front - contract_rows(factor_rows, factor_cols))
 
 

time: 279 us -> 295 us (1.057)
  waiting for transfers between devices: 228 us -> 237 us
  other arithmetic: 5.59 us -> 10.3 us
    all_gather x0 -> x1, waiting for transfers between devices: none -> 66.3 us  [local(): lax.all_gather(kept.astype(jnp.bfloat16), 'grid')]
    psum x1 -> x0, waiting for transfers between devices: 57 us -> none  [local(): factor_rows = lax.psum(kept.astype(jnp.bfloat16), 'grid')]
    reduce_sum x0 -> x1, other arithmetic: none -> 4.72 us  [local(): jnp.sum(lax.all_gather(kept.astype(jnp.bfloat16), 'grid'), axis=0)]
where the time goes in v2:
time: 295 us
  waiting for transfers between devices  237 us (80%)
  matrix products  27.4 us (9%)
  between operations  15.9 us (5%)
  other arithmetic  10.3 us (3%)
  local copies, waits for them, and re-layouts  3.71 us (1%)
    reduce_scatter x1, waiting for transfers between devices, local(): lax.psum_scatter(partial_value, 'obs', scatter_dimension=0, tiled=True)  83.4 us
    all_gather x1, waiting for transfers between devices, local(): lax.all_gather(kept.astype(jnp.bfloat16), 'grid')  66.3 us
    all_gather x1, waiting for transfers between devices, local(): lax.all_gather(block_part, ('team', 'obs'), axis=0, tiled=True)  41.5 us
    all_gather x1, waiting for transfers between devices, local(): panel_piece = lax.all_gather(design_panel, 'grid', axis=1, tiled=True)  37.6 us
    dot_general x2, matrix products, contract_rows(): lax.dot_general(left, right, (((0,), (0,)), ((), ())), preferred_element_...  15.5 us
    dot_general x1, matrix products, local(): jnp.dot(inverse_whole, jnp.concatenate([block_whole, block_whole], axis=0...  11.9 us
    all_gather x1, waiting for transfers between devices, local(): inverse_whole = lax.all_gather(split, ('team', 'obs'), axis=0, tiled=True)  7.5 us
  transfers between devices with their start and end apart: 5, of which 5 were waited for; matrix products, arithmetic and copies ran while one was open for 2% of the time, Pallas kernels for 0%

profile of v2, /device:TPU:0, one launch (start us, length us, event | category | flops | bytes accessed | tf_op | source)
XLA Modules:
  0.0 294.7 jit_solution(18253196429031519960)
XLA Ops:
  8.0 0.0 all-gather.8.cloned.1.call-start
  8.0 0.7 all-gather.8.cloned.1.call-update
  8.7 0.0 reduce-scatter.2.cloned.1.call-start
  9.4 1.3 select_reduce_fusion
  10.8 0.0 copy-start.1
  10.8 37.6 %all-gather.8.cloned.1.call-done = bf16[2048,512]{1,0:T(8,128)(2,1)} async-done(((bf16[2048,128]{1,0:T(8,128)(2,1)}), bf16[2048,512]{1,0:T(8,128)(2,1)}) %all-gather.8.cloned.1.call-update) | async-done | bytes 2097168 | tf_op jit(solution)/shard_map/all_gather | solution.py:28
  48.4 8.6 %fusion.6 = f32[512,1536]{0,1:T(8,128)} fusion(bf16[2048,512]{1,0:T(8,128)(2,1)} %all-gather.8.cloned.1.call-done, bf16[2048,1536]{1,0:T(8,128)(2,1)} %param.8, f32[2048]{0:T(1024)S(1)} %fusion.8), kind=kOutput, calls=%fused_computation.8 | convolution fusion | flops 3230662656 | bytes 11542528 | tf_op jit(solution)/shard_map/dot_general | solution.py:17
  57.1 0.0 reduce-scatter.2.cloned.1.call-update
  57.1 0.0 all-gather.6.cloned.1.call-start
  57.2 0.0 copy-done.1
  57.2 0.1 reduce-precision_convert_fusion
  57.3 0.8 pad_maximum_fusion
  58.1 0.0 all-gather.6.cloned.1.call-update
  58.1 0.0 all-gather.10.cloned.1.call-start
  58.2 83.4 %reduce-scatter.2.cloned.1.call-done = f32[128,1536]{0,1:T(8,128)} async-done(((f32[512,1536]{0,1:T(8,128)}), f32[128,1536]{0,1:T(8,128)}) %reduce-scatter.2.cloned.1.call-update) | async-done | bytes 786448 | tf_op jit(solution)/shard_map/reduce_scatter | solution.py:32
  141.5 1.9 convert_element_type.20
  143.5 0.0 all-gather.10.cloned.1.call-update
  143.5 0.0 all-gather.12.cloned.1.call-start
  143.6 7.5 %all-gather.6.cloned.1.call-done = bf16[1024,2048]{1,0:T(8,128)(2,1)} async-done(((bf16[128,2048]{1,0:T(8,128)(2,1)}), bf16[1024,2048]{1,0:T(8,128)(2,1)}) %all-gather.6.cloned.1.call-update) | async-done | bytes 4194320 | tf_op jit(solution)/shard_map/all_gather | solution.py:25
  151.1 41.5 %all-gather.10.cloned.1.call-done = bf16[1024,1536]{0,1:T(8,128)(2,1)} async-done(((bf16[128,1536]{0,1:T(8,128)(2,1)}), bf16[1024,1536]{0,1:T(8,128)(2,1)}) %all-gather.10.cloned.1.call-update) | async-done | bytes 3145744 | tf_op jit(solution)/shard_map/all_gather | solution.py:34
  192.6 11.9 %fusion.10 = (bf16[1024,1536]{1,0:T(8,128)(2,1)S(1)}, f32[1024,1536]{1,0:T(8,128)}) fusion(bf16[1024,2048]{1,0:T(8,128)(2,1)} %all-gather.6.cloned.1.call-done, bf16[1024,1536]{0,1:T(8,128)(2,1)} %all-gather.10.cloned.1.call-done), kind=kOutput, calls=%fused_computation.20 | convolution fusion | flops 6456606720 | bytes 16777216 | tf_op jit(solution)/shard_map/dot_general | solution.py:35
  204.5 0.0 copy-start
  204.5 1.6 copy-done
  206.1 1.4 dynamic-slice_select_fusion
  207.5 0.0 all-gather.12.cloned.1.call-update
  207.5 2.1 constant_dynamic-slice_fusion
  209.6 66.3 %all-gather.12.cloned.1.call-done = bf16[4096,768]{1,0:T(8,128)(2,1)} async-done(((bf16[1024,768]{1,0:T(8,128)(2,1)}), bf16[4096,768]{1,0:T(8,128)(2,1)}) %all-gather.12.cloned.1.call-update) | async-done | bytes 6291472 | tf_op jit(solution)/shard_map/all_gather | solution.py:47
  275.9 4.7 %reduce_sum.22 = bf16[1024,768]{1,0:T(8,128)(2,1)S(1)} reduce(bf16[4,1024,768]{2,1,0:T(8,128)(2,1)} %bitcast.9, bf16[]{:T(256)} %constant.53.clone.1), dimensions={0}, to_apply=%region_2.3 | reduce | flops 2359296 | bytes 7864322 | tf_op jit(solution)/shard_map/reduce_sum | solution.py:47
  280.7 6.9 %convolution_subtract_fusion = f32[768,1536]{1,0:T(8,128)} fusion(f32[768,1536]{1,0:T(8,128)} %param.13, bf16[1024,768]{1,0:T(8,128)(2,1)S(1)} %reduce_sum.22, bf16[1024,1536]{1,0:T(8,128)(2,1)} %copy-done), kind=kOutput, calls=%fused_computation.7 | convolution fusion | flops 2417098752 | bytes 14155776 | tf_op jit(solution)/shard_map/dot_general | solution.py:17
  (1 shorter events, 0.0 us)
Async XLA Ops:
  8.0 40.4 %all-gather.8.cloned.1.call-start = ((), (), s32[]{:S(2)}) async-start(), calls=%async_computation.2 | async-start | bytes 2621440 | tf_op jit(solution)/shard_map/all_gather | solution.py:28
  8.7 132.8 %reduce-scatter.2.cloned.1.call-start = ((), (), s32[]{:S(2)}) async-start(), calls=%async_computation.3 | async-start | bytes 3932160 | tf_op jit(solution)/shard_map/reduce_scatter | solution.py:32
  10.8 46.4 %copy-start.1 = (f32[128,1024]{1,0:T(8,128)S(1)}, f32[128,1024]{1,0:T(8,128)}, u32[]{:S(2)}) copy-start(f32[128,1024]{1,0:T(8,128)} %param.12) | copy-start | bytes 1572868
  57.1 94.0 %all-gather.6.cloned.1.call-start = ((), (), s32[]{:S(2)}) async-start(), calls=%async_computation.1 | async-start | bytes 4718592 | tf_op jit(solution)/shard_map/all_gather | solution.py:25
  58.1 134.5 %all-gather.10.cloned.1.call-start = ((), (), s32[]{:S(2)}) async-start(), calls=%async_computation.4 | async-start | bytes 3538944 | tf_op jit(solution)/shard_map/all_gather | solution.py:34
  143.5 132.5 %all-gather.12.cloned.1.call-start = ((), (), s32[]{:S(2)}) async-start(), calls=%async_computation.5 | async-start | bytes 7864320 | tf_op jit(solution)/shard_map/all_gather | solution.py:47
  204.5 1.6 copy-start
Sparse Core Ops, SparseCore 0:
  10.6 37.7 all-gather.7
  57.2 84.2 reduce-scatter.1
  207.6 68.2 all-gather.11
Sparse Core Ops, SparseCore 1:
  59.8 91.3 all-gather.5
  153.1 39.4 all-gather.9
